TPU v7x, 256 devices: a whole 4x4x8 slice. The times are simulated.
256 devices in a mesh: freq: 128 (over x, y, z_hi, core), plane: 2 (over z_lo).
Axes of the slice: x: 4, y: 4, z: 8 (z_hi: 4, z_lo: 2; z = z_hi * 2 + z_lo), core: 2. Of those that a mesh axis runs over, the one named last changes fastest.
Arguments:
- state_in: float32 [2, 256, 5, 256, 128], P(None, 'freq', None, 'plane'), may hold values from -6 to 6
- forcing_in: float32 [2, 256, 5, 256, 128], P(None, 'freq', None, 'plane'), may hold values from -6 to 6
- base_flow: float32 [128, 5, 256, 128], P('freq', None, 'plane'), may hold values from -1 to 1
- station_index: int32 [2], replicated, may hold values from 0 to 127
- lobe_count: int32 [1], replicated, may hold values from 3 to 127
Outputs:
- state_out: float32 [2, 256, 5, 256, 128], P(None, 'freq', None, 'plane')
- forcing_out: float32 [2, 256, 5, 256, 128], P(None, 'freq', None, 'plane')
All inputs are finite; a program needn't handle non-finite values.
Results may differ from a plain program's by a relative error of at most 0.0003.
Values sent between devices are 32-bit elements; how exact they have to be, the bound alone decides.
No kernel may reach another device: no remote copies, remote signals or barrier semaphores. Data moves between devices by JAX's collectives and lax.ppermute only.
A program may use at most 128 MiB of HBM per device.

v0:
```python
import math
import jax
import jax.numpy as jnp
from jax import lax
from jax.sharding import PartitionSpec as P

SWEEPS = 4
STEPS = 2
SIDE_WEIGHT = 1.25
MARCH_WEIGHT = 4.0
DIAG_SHIFT = 4.0
ADVECT_SCALE = 0.5
BASE_SCALE = 0.5
HIGHEST_MODE = lax.Precision.HIGHEST


def broadcast(value, axis, source):
    kept = jnp.where(lax.axis_index(axis) == source, value, 0).astype(value.dtype)
    return lax.psum(kept, axis)


def padded_2(cells, sides, width):
    for axis, dim in sides:
        count = lax.axis_size(axis)
        head = lax.slice_in_dim(cells, 0, width, axis=dim)
        tail = lax.slice_in_dim(cells, cells.shape[dim] - width, cells.shape[dim], axis=dim)
        cells = jnp.concatenate(
            [
                lax.ppermute(tail, axis, [(i, (i + 1) % count) for i in range(count)]),
                cells,
                lax.ppermute(head, axis, [((i + 1) % count, i) for i in range(count)]),
            ],
            axis=dim,
        )
    return cells


def radial_tables(radius_count):
    indices = jnp.arange(radius_count)
    angles = math.pi * indices.astype(jnp.float32) / (radius_count - 1)
    cheb_nodes = jnp.cos(angles)
    weights = jnp.where((indices == 0) | (indices == radius_count - 1), 2.0, 1.0).astype(
        jnp.float32
    )
    parity = (1 - 2 * ((indices[:, None] + indices[None, :]) % 2)).astype(jnp.float32)
    offdiag = indices[:, None] != indices[None, :]
    spacing = jnp.where(offdiag, cheb_nodes[:, None] - cheb_nodes[None, :], 1.0)
    entries = jnp.where(offdiag, weights[:, None] / weights[None, :] * parity / spacing, 0.0)
    entries = entries - jnp.diag(jnp.sum(entries, axis=1))
    slopes = jnp.sin(angles)[:, None] * entries / (radius_count - 1)
    stiffness = jnp.dot(slopes.T, slopes, precision=HIGHEST_MODE)
    system = stiffness + DIAG_SHIFT * jnp.eye(radius_count, dtype=jnp.float32)
    factor = jnp.linalg.cholesky(system)
    factor_inv = lax.linalg.triangular_solve(
        factor, jnp.eye(radius_count, dtype=jnp.float32), left_side=True, lower=True
    )
    return (slopes, jnp.dot(factor_inv.T, factor_inv, precision=HIGHEST_MODE))


def transform_tables(freqs, ntime):
    mode_ids = jnp.arange(freqs)
    time_ids = jnp.arange(ntime)
    phases = mode_ids[:, None] * time_ids[None, :] % ntime
    angles = 2.0 * math.pi * phases.astype(jnp.float32) / ntime
    cosines = jnp.cos(angles)
    sine_tab = jnp.sin(angles)
    stacked = jnp.concatenate([cosines, -sine_tab], axis=0)
    return (stacked.T / math.sqrt(freqs), stacked / math.sqrt(ntime))


def chevron(lobe_count, azimuths, start_az, total_az):
    position = start_az + jnp.arange(azimuths)
    phases = lobe_count[0] * position % total_az
    return 1.0 + 0.5 * jnp.cos(2.0 * math.pi * phases.astype(jnp.float32) / total_az)


def relax_sweep(inner, neighbours, right_side, coefficient, omegas, inverse_p):
    real_part = inner[0]
    imag_part = inner[1]
    rate_col = omegas[:, None, None, None]
    scaled = coefficient[None]
    mixing = jnp.stack(
        [scaled * real_part - rate_col * imag_part, scaled * imag_part + rate_col * real_part]
    )
    summed = right_side - mixing + SIDE_WEIGHT * neighbours
    radius_count = summed.shape[-1]
    return jnp.dot(summed.reshape(-1, radius_count), inverse_p.T, precision=HIGHEST_MODE).reshape(
        summed.shape
    )


def advect(velocity, radial_time, around_time):
    carried = velocity[:, 1:2] * radial_time + velocity[:, 2:3] * around_time
    spread = velocity[:, 0] * (radial_time[:, 1] + around_time[:, 2])
    carried = jnp.concatenate([carried[:, 0:1] + spread[:, None], carried[:, 1:]], axis=1)
    return -ADVECT_SCALE * carried


def per_device(state_in, forcing_in, base_flow, station_index, lobe_count):
    per_dev = state_in.shape[1]
    variables = state_in.shape[2]
    span_az = state_in.shape[3]
    radius_count = state_in.shape[4]
    freqs = per_dev * lax.axis_size("freq")
    ntime = 3 * freqs // 2
    slopes, inverse_p = radial_tables(radius_count)
    inverse, forward = transform_tables(freqs, ntime)
    first_mode = lax.axis_index("freq") * per_dev
    omegas = 0.5 * (first_mode + jnp.arange(per_dev)).astype(jnp.float32) / freqs
    shape_az = chevron(
        lobe_count, span_az, lax.axis_index("plane") * span_az, span_az * lax.axis_size("plane")
    )
    stored = base_flow.shape[0]
    march_state = state_in
    forcing = forcing_in
    for station in range(STEPS):
        wanted = station_index[station]
        local_plane = lax.dynamic_index_in_dim(base_flow, wanted % stored, 0, keepdims=False)
        plane_flow = broadcast(local_plane, "freq", wanted // stored)
        coefficient = BASE_SCALE * plane_flow * shape_az[None, :, None]
        right_side = MARCH_WEIGHT * march_state + forcing
        iterate = march_state
        for sweep_no in range(SWEEPS):
            padded = padded_2(iterate, (("plane", 3),), 1)
            iterate = relax_sweep(
                iterate,
                padded[:, :, :, 2:] + padded[:, :, :, :-2],
                right_side,
                coefficient,
                omegas,
                inverse_p,
            )
        march_state = iterate
        rimmed = padded_2(march_state, (("plane", 3),), 1)
        beside_all = 0.5 * (rimmed[:, :, :, 2:] - rimmed[:, :, :, :-2])
        radial = jnp.dot(
            march_state.reshape(-1, radius_count), slopes.T, precision=HIGHEST_MODE
        ).reshape(march_state.shape)
        fields = jnp.stack([march_state, radial, beside_all])
        points = lax.all_to_all(fields, "freq", split_axis=4, concat_axis=2, tiled=True)
        in_time = jnp.einsum(
            "tc,kcx->ktx", inverse, points.reshape(3, 2 * freqs, -1), precision=HIGHEST_MODE
        ).reshape(3, ntime, variables, -1)
        velocity = in_time[0]
        radial_time = in_time[1]
        around_time = in_time[2]
        source = advect(velocity, radial_time, around_time)
        spectral = jnp.dot(forward, source.reshape(ntime, -1), precision=HIGHEST_MODE).reshape(
            2, freqs, variables, -1, radius_count
        )
        forcing = lax.all_to_all(spectral, "freq", split_axis=1, concat_axis=3, tiled=True)
    return (march_state, forcing)


def solution(mesh):
    return jax.shard_map(
        per_device,
        mesh=mesh,
        in_specs=(
            P(None, "freq", None, "plane", None),
            P(None, "freq", None, "plane", None),
            P("freq", None, "plane", None),
            P(),
            P(),
        ),
        out_specs=(P(None, "freq", None, "plane", None), P(None, "freq", None, "plane", None)),
        check_vma=False,
    )
```

profile of v0, /device:TPU:32, one launch (start us, length us, event | category | flops | bytes accessed | tf_op | source)
XLA Modules:
  0.0 1701.8 jit_solution(14322298090802658548)
XLA Ops:
  8.2 1.9 collective-permute-start
  10.3 1.3 fusion.125
  12.9 1.9 select_bitcast_fusion
  16.3 11.7 cholesky.18
  29.4 9.8 custom-call.6
  39.8 1249.7 %all-reduce.3.cloned.1.call-done = (f32[5,128,128]{2,1,0:T(8,128)}, f32[5,128,128]{2,1,0:T(8,128)}) async-done(((f32[5,128,128]{2,1,0:T(8,128)}, f32[5,128,128]{2,1,0:T(8,128)}), (f32[5,128,128]{2,1,0:T(8,128)}, f32[5,128,128]{2,1,0:T(8,128)})) %all-reduce.3.cloned.1.call-update) | async-done | bytes 655376 | tf_op jit(solution)/shard_map/psum | solution.py:19
  1289.5 1.2 broadcast_multiply_fusion
  1293.8 1.5 collective-permute-start.2
  1297.6 1.8 collective-permute-done.3
  1299.9 1.2 fusion.128
  1302.0 1.4 collective-permute-start.5
  1303.7 1.3 collective-permute-done.4
  1307.5 1.5 collective-permute-start.6
  1310.0 1.3 collective-permute-done.6
  1311.3 1.4 collective-permute-done.7
  1315.2 1.5 collective-permute-start.9
  1316.7 1.3 fusion.67
  1319.7 4.9 copy.116
  1324.6 7.3 all-to-all-start
  1331.9 1.6 sine_negate_fusion
  1333.6 75.5 %all-to-all-done = f32[3,2,2,5,128,128]{5,2,3,1,0,4:T(2,128)} async-done(((f32[3,2,2,5,128,128]{5,2,3,1,0,4:T(2,128)}), f32[3,2,2,5,128,128]{5,2,3,1,0,4:T(2,128)}, u32[]{:S(2)}, u32[]{:S(2)}) %all-to-all-start) | async-done | bytes 3932192 | tf_op jit(solution)/shard_map/all_to_all | solution.py:140
  1409.2 5.6 copy.117
  1414.8 6.8 reshape.545
  1421.6 8.6 convolution_bitcast_fusion.1
  1430.8 2.5 convolution_bitcast_fusion.3
  1433.3 2.1 copy.119
  1435.4 21.5 %all-to-all-start.1 = ((f32[2,256,5,1,128]{4,0,3,2,1:T(2,128)}), f32[2,256,5,1,128]{4,0,3,2,1:T(2,128)S(1)}, u32[]{:S(2)}, u32[]{:S(2)}) async-start(f32[2,256,5,1,128]{4,0,3,2,1:T(2,128)} %copy.119), calls=%async_computation.1 | async-start | bytes 2621440 | tf_op jit(solution)/shard_map/all_to_all | solution.py:151
  1457.0 1.3 multiply_subtract_fusion.3
  1458.3 30.5 %all-to-all-done.1 = f32[2,256,5,1,128]{4,0,3,2,1:T(2,128)S(1)} async-done(((f32[2,256,5,1,128]{4,0,3,2,1:T(2,128)}), f32[2,256,5,1,128]{4,0,3,2,1:T(2,128)S(1)}, u32[]{:S(2)}, u32[]{:S(2)}) %all-to-all-start.1) | async-done | bytes 1310752 | tf_op jit(solution)/shard_map/all_to_all | solution.py:151
  1488.9 1.7 fusion.24
  1491.9 7.1 collective-permute-start.10
  1499.5 1.2 collective-permute-done.10
  1500.7 2.0 collective-permute-done.11
  1504.7 1.9 collective-permute-start.13
  1507.0 1.3 collective-permute-done.12
  1510.2 2.0 collective-permute-start.14
  1514.0 2.1 collective-permute-done.15
  1516.6 1.2 fusion.134
  1518.0 1.9 collective-permute-start.17
  1519.9 1.3 fusion.66
  1522.2 3.0 copy.122
  1525.3 99.7 %all_to_all.66 = f32[3,2,2,5,128,128]{5,2,3,1,0,4:T(2,128)S(1)} all-to-all(f32[3,2,2,5,128,128]{5,2,3,1,0,4:T(2,128)S(1)} %copy.122), channel_id=1, replica_groups=mesh['freq'=128,'plane'=2] {'freq'}, dimensions={4} | all-to-all | bytes 7864320 | tf_op jit(solution)/shard_map/all_to_all | solution.py:140
  1624.9 3.5 copy.123
  1628.4 6.9 reshape.555
  1635.3 8.6 convolution_bitcast_fusion
  1645.5 2.5 convolution_bitcast_fusion.2
  1649.1 44.3 %all_to_all.67 = f32[2,256,5,1,128]{4,0,3,2,1:T(2,128)S(1)} all-to-all(f32[2,256,5,1,128]{4,0,3,2,1:T(2,128)S(1)} %copy.125), channel_id=1, replica_groups=mesh['freq'=128,'plane'=2] {'freq'}, dimensions={1} | all-to-all | bytes 2621440 | tf_op jit(solution)/shard_map/all_to_all | solution.py:151
  1693.3 1.2 copy.142
  (100 shorter events, 31.0 us)
Async XLA Ops:
  7.2 1282.3 %all-reduce.3.cloned.1.call-start = ((), (), s32[]{:S(2)}) async-start(), calls=%async_computation.4 | async-start | bytes 1310720 | tf_op jit(solution)/shard_map/psum | solution.py:19
  8.2 1282.9 %collective-permute-start = (f32[2,2,5,1,128]{4,3,2,1,0:T(1,128)S(1)}, f32[2,2,5,1,128]{4,3,2,1,0:T(1,128)S(1)}, u32[]{:S(2)}, u32[]{:S(2)}) collective-permute-start(f32[2,2,5,1,128]{4,3,2,1,0:T(1,128)S(1)} %get-tuple-element.56), channel_id=1, source_target_pairs={{1,0},{0,1},{3,2},{2,3},{5,4},{4,5},{7,6},{6,7},{9,8},{8,9},{11,10... | collective-permute-start | bytes 30728 | tf_op jit(solution)/shard_map/ppermute | solution.py:31
  10.1 1281.0 %collective-permute-start.1 = (f32[2,2,5,1,128]{4,3,2,1,0:T(1,128)S(1)}, f32[2,2,5,1,128]{4,3,2,1,0:T(1,128)S(1)}, u32[]{:S(2)}, u32[]{:S(2)}) collective-permute-start(f32[2,2,5,1,128]{4,3,2,1,0:T(1,128)S(1)} %get-tuple-element.57), channel_id=1, source_target_pairs={{0,1},{1,0},{2,3},{3,2},{4,5},{5,4},{6,7},{7,6},{8,9},{9,8},{10,11... | collective-permute-start | bytes 30728 | tf_op jit(solution)/shard_map/ppermute | solution.py:29
  16.1 1274.5 %copy-start = (f32[2,2,5,128,128]{4,3,2,1,0:T(8,128)S(1)}, f32[2,2,5,128,128]{4,3,2,1,0:T(8,128)}, u32[]{:S(2)}) copy-start(f32[2,2,5,128,128]{4,3,2,1,0:T(8,128)} %param.5) | copy-start | bytes 3932164
  1290.7 1.3 copy-start.2
  1293.8 3.8 collective-permute-start.2
  1295.3 4.1 collective-permute-start.3
  1301.2 3.8 collective-permute-start.4
  1302.0 3.7 collective-permute-start.5
  1307.5 3.8 collective-permute-start.6
  1309.0 3.7 collective-permute-start.7
  1314.4 3.8 collective-permute-start.8
  1315.2 3.8 collective-permute-start.9
  1324.6 84.6 %all-to-all-start = ((f32[3,2,2,5,128,128]{5,2,3,1,0,4:T(2,128)}), f32[3,2,2,5,128,128]{5,2,3,1,0,4:T(2,128)}, u32[]{:S(2)}, u32[]{:S(2)}) async-start(f32[3,2,2,5,128,128]{5,2,3,1,0,4:T(2,128)} %copy.116), calls=%async_computation | async-start | bytes 7864320 | tf_op jit(solution)/shard_map/all_to_all | solution.py:140
  1333.5 88.1 %copy-start.5 = (f32[256,384]{1,0:T(8,128)}, f32[256,384]{1,0:T(8,128)S(1)}, u32[]{:S(2)}) copy-start(f32[256,384]{1,0:T(8,128)S(1)} %get-tuple-element.71) | copy-start | bytes 1179652
  1333.6 97.2 %copy-start.3 = (f32[512,384]{1,0:T(8,128)}, f32[512,384]{1,0:T(8,128)S(1)}, u32[]{:S(2)}) copy-start(f32[512,384]{1,0:T(8,128)S(1)} %fusion.37) | copy-start | bytes 2359300
  1435.4 53.5 %all-to-all-start.1 = ((f32[2,256,5,1,128]{4,0,3,2,1:T(2,128)}), f32[2,256,5,1,128]{4,0,3,2,1:T(2,128)S(1)}, u32[]{:S(2)}, u32[]{:S(2)}) async-start(f32[2,256,5,1,128]{4,0,3,2,1:T(2,128)} %copy.119), calls=%async_computation.1 | async-start | bytes 2621440 | tf_op jit(solution)/shard_map/all_to_all | solution.py:151
  1491.9 8.8 collective-permute-start.10
  1499.1 3.7 collective-permute-start.11
  1504.5 3.8 collective-permute-start.12
  1504.7 3.7 collective-permute-start.13
  1510.2 3.8 collective-permute-start.14
  1512.2 3.9 collective-permute-start.15
  1517.8 4.2 copy-start.1
  1517.8 3.8 collective-permute-start.16
  1518.0 3.7 collective-permute-start.17
  1628.4 6.9 copy-start.6
  1644.4 1.1 copy-start.4
Sparse Core Ops, SparseCore 0:
  14.9 1274.5 all-reduce.2
where the time goes:
time: 1710 us; the launch traced here: 1700 us
  waiting for transfers between devices  1370 us (80%)
  blocking collectives  144 us (8%)
  starting transfers between devices  53.8 us (3%)
  local copies, waits for them, and re-layouts  40.7 us (2%)
  other arithmetic  38.3 us (2%)
  matrix products  35.5 us (2%)
    psum x1, waiting for transfers between devices, broadcast(): return lax.psum(kept, axis)  1250 us
    all_to_all x1, blocking collectives, per_device(): lax.all_to_all(fields, 'freq', split_axis=4, concat_axis=2, tiled=True)  99.7 us
    all_to_all x1, waiting for transfers between devices, per_device(): lax.all_to_all(fields, 'freq', split_axis=4, concat_axis=2, tiled=True)  75.5 us
    all_to_all x1, blocking collectives, per_device(): lax.all_to_all(spectral, 'freq', split_axis=1, concat_axis=3, tiled=True)  44.3 us
  transfers between devices with their start and end apart: 21, of which 19 were waited for; matrix products, arithmetic and copies ran while one was open for 2% of the time, Pallas kernels for 0%

commit v1 on v0

--- a/solution.py
+++ b/solution.py
@@ -16,7 +16,7 @@
 
 def broadcast(value, axis, source):
     kept = jnp.where(lax.axis_index(axis) == source, value, 0).astype(value.dtype)
-    return lax.psum(kept, axis)
+    return jnp.sum(lax.all_gather(kept, axis), axis=0)
 
 
 def padded_2(cells, sides, width):

time: 1710 us -> 859 us (0.50)
  waiting for transfers between devices: 1370 us -> 485 us
  other arithmetic: 38.3 us -> 66.6 us
    psum x1 -> x0, waiting for transfers between devices: 1250 us -> none  [broadcast(): return lax.psum(kept, axis)]
    all_gather x0 -> x2, waiting for transfers between devices: none -> 364 us  [broadcast(): return jnp.sum(lax.all_gather(kept, axis), axis=0)]
    reduce_sum x0 -> x2, other arithmetic: none -> 29.4 us  [broadcast(): return jnp.sum(lax.all_gather(kept, axis), axis=0)]
  transfers between devices with their start and end apart: 21 -> 22, of which waited for: 19 -> 20; matrix products, arithmetic and copies ran while one was open for 2% -> 7% of each run, Pallas kernels for 0% -> 0%
where the time goes in v1:
time: 859 us; the launch traced here: 850 us
  waiting for transfers between devices  485 us (56%)
  blocking collectives  144 us (17%)
  other arithmetic  66.6 us (8%)
  starting transfers between devices  61.8 us (7%)
  local copies, waits for them, and re-layouts  39.8 us (5%)
  matrix products  35.4 us (4%)
  between operations  17 us (2%)
    all_gather x2, waiting for transfers between devices, broadcast(): return jnp.sum(lax.all_gather(kept, axis), axis=0)  364 us
    all_to_all x1, blocking collectives, per_device(): lax.all_to_all(fields, 'freq', split_axis=4, concat_axis=2, tiled=True)  100 us
    all_to_all x1, waiting for transfers between devices, per_device(): lax.all_to_all(fields, 'freq', split_axis=4, concat_axis=2, tiled=True)  72.2 us
    all_to_all x1, blocking collectives, per_device(): lax.all_to_all(spectral, 'freq', split_axis=1, concat_axis=3, tiled=True)  44.3 us
    all_to_all x1, waiting for transfers between devices, per_device(): lax.all_to_all(spectral, 'freq', split_axis=1, concat_axis=3, tiled=True)  30.4 us
    reduce_sum x2, other arithmetic, broadcast(): return jnp.sum(lax.all_gather(kept, axis), axis=0)  29.4 us
    all_to_all x1, starting transfers between devices, per_device(): lax.all_to_all(spectral, 'freq', split_axis=1, concat_axis=3, tiled=True)  24.9 us
    dot_general x2, matrix products, per_device(): jnp.einsum('tc,kcx->ktx', inverse, points.reshape(3, 2 * freqs, -1), prec...  17.3 us
  transfers between devices with their start and end apart: 22, of which 20 were waited for; matrix products, arithmetic and copies ran while one was open for 7% of the time, Pallas kernels for 0%

profile of v1, /device:TPU:32, one launch (start us, length us, event | category | flops | bytes accessed | tf_op | source)
XLA Modules:
  0.0 849.7 jit_solution(8460665189627302789)
XLA Ops:
  7.2 1.3 fusion.125
  9.9 1.9 broadcast_select_fusion
  12.5 1.9 collective-permute-start.1
  16.2 11.7 %cholesky.18 = f32[128,128]{1,0:T(8,128)S(1)} custom-call(f32[128,128]{1,0:T(8,128)S(1)} %fusion.64), custom_call_target="Cholesky" | custom-call | tf_op jit(solution)/shard_map/jit(cholesky)/cholesky | solution.py:53
  29.1 9.8 %custom-call.6 = f32[1,128,128]{1,2,0:T(8,128)S(1)} custom-call(f32[1,128,128]{2,1,0:T(8,128)S(1)} %fusion.56), custom_call_target="InvertDiagBlocksLowerTriangular" | custom-call | tf_op jit(solution)/shard_map/triangular_solve | solution.py:54
  39.5 175.4 %all-gather.5.cloned.1.call-done = f32[128,5,128,128]{3,2,1,0:T(8,128)} async-done(((f32[1,5,128,128]{3,2,1,0:T(8,128)}), f32[128,5,128,128]{3,2,1,0:T(8,128)}) %all-gather.5.cloned.1.call-update) | async-done | bytes 41943056 | tf_op jit(solution)/shard_map/all_gather | solution.py:19
  215.0 14.7 %reduce_sum.29 = f32[5,128,128]{2,1,0:T(8,128)S(1)} reduce(f32[128,5,128,128]{3,2,1,0:T(8,128)} %all-gather.5.cloned.1.call-done, f32[]{:T(128)} %constant.158.clone.1), dimensions={0}, to_apply=%region_4.5 | reduce | flops 10403840 | bytes 42270724 | tf_op jit(solution)/shard_map/reduce_sum | solution.py:19
  229.7 189.0 %all-gather.3.cloned.1.call-done = f32[128,5,128,128]{3,2,1,0:T(8,128)} async-done(((f32[1,5,128,128]{3,2,1,0:T(8,128)}), f32[128,5,128,128]{3,2,1,0:T(8,128)}) %all-gather.3.cloned.1.call-update) | async-done | bytes 41943056 | tf_op jit(solution)/shard_map/all_gather | solution.py:19
  418.7 14.7 %reduce_sum.27 = f32[5,128,128]{2,1,0:T(8,128)S(1)} reduce(f32[128,5,128,128]{3,2,1,0:T(8,128)} %all-gather.3.cloned.1.call-done, f32[]{:T(128)} %constant.158.clone.1), dimensions={0}, to_apply=%region_0.1 | reduce | flops 10403840 | bytes 42270724 | tf_op jit(solution)/shard_map/reduce_sum | solution.py:19
  437.2 1.9 collective-permute-start.2
  443.2 1.6 collective-permute-start.5
  445.7 1.3 collective-permute-done.5
  447.0 1.5 collective-permute-done.4
  451.0 1.5 collective-permute-start.6
  452.8 1.3 collective-permute-done.7
  456.4 1.6 collective-permute-start.8
  458.7 1.3 fusion.67
  460.2 1.6 collective-permute-done.9
  462.5 4.9 copy.114
  467.4 11.7 %all-to-all-start = ((f32[3,2,2,5,128,128]{5,2,3,1,0,4:T(2,128)}), f32[3,2,2,5,128,128]{5,2,3,1,0,4:T(2,128)}, u32[]{:S(2)}, u32[]{:S(2)}) async-start(f32[3,2,2,5,128,128]{5,2,3,1,0,4:T(2,128)} %copy.114), calls=%async_computation | async-start | bytes 7864320 | tf_op jit(solution)/shard_map/all_to_all | solution.py:140
  479.1 1.6 sine_negate_fusion
  480.8 72.2 %all-to-all-done = f32[3,2,2,5,128,128]{5,2,3,1,0,4:T(2,128)} async-done(((f32[3,2,2,5,128,128]{5,2,3,1,0,4:T(2,128)}), f32[3,2,2,5,128,128]{5,2,3,1,0,4:T(2,128)}, u32[]{:S(2)}, u32[]{:S(2)}) %all-to-all-start) | async-done | bytes 3932192 | tf_op jit(solution)/shard_map/all_to_all | solution.py:140
  553.1 5.6 copy.115
  558.7 6.8 reshape.543
  565.5 8.6 %convolution_bitcast_fusion.1 = f32[3,384,640]{1,2,0:T(8,128)S(1)} fusion(f32[3,512,640]{2,1,0:T(8,128)} %reshape.543, f32[256,384]{1,0:T(8,128)S(1)} %get-tuple-element.68, f32[256,384]{1,0:T(8,128)S(1)} %get-tuple-element.69), kind=kOutput, calls=%fused_computation.3 | convolution fusion | flops 4530241536 | bytes 7667712 | tf_op jit(solution)/shard_map/tc,kcx->ktx/dot_general | solution.py:141
  574.7 2.5 convolution_bitcast_fusion.3
  577.2 2.1 copy.117
  579.3 24.9 %all-to-all-start.1 = ((f32[2,256,5,1,128]{4,0,3,2,1:T(2,128)}), f32[2,256,5,1,128]{4,0,3,2,1:T(2,128)S(1)}, u32[]{:S(2)}, u32[]{:S(2)}) async-start(f32[2,256,5,1,128]{4,0,3,2,1:T(2,128)} %copy.117), calls=%async_computation.1 | async-start | bytes 2621440 | tf_op jit(solution)/shard_map/all_to_all | solution.py:151
  604.3 1.3 multiply_subtract_fusion.3
  605.6 30.4 %all-to-all-done.1 = f32[2,256,5,1,128]{4,0,3,2,1:T(2,128)S(1)} async-done(((f32[2,256,5,1,128]{4,0,3,2,1:T(2,128)}), f32[2,256,5,1,128]{4,0,3,2,1:T(2,128)S(1)}, u32[]{:S(2)}, u32[]{:S(2)}) %all-to-all-start.1) | async-done | bytes 1310752 | tf_op jit(solution)/shard_map/all_to_all | solution.py:151
  636.0 1.7 fusion.24
  639.0 7.3 collective-permute-start.11
  646.8 1.2 collective-permute-done.11
  648.0 2.0 collective-permute-done.10
  652.0 1.9 collective-permute-start.12
  654.3 1.3 collective-permute-done.13
  657.5 2.0 collective-permute-start.15
  661.2 2.2 collective-permute-done.14
  665.2 2.0 collective-permute-start.16
  667.2 1.3 fusion.66
  669.7 3.0 copy.120
  672.7 100.2 %all_to_all.66 = f32[3,2,2,5,128,128]{5,2,3,1,0,4:T(2,128)S(1)} all-to-all(f32[3,2,2,5,128,128]{5,2,3,1,0,4:T(2,128)S(1)} %copy.120), channel_id=1, replica_groups=mesh['freq'=128,'plane'=2] {'freq'}, dimensions={4} | all-to-all | bytes 7864320 | tf_op jit(solution)/shard_map/all_to_all | solution.py:140
  772.9 3.5 copy.121
  776.4 6.9 reshape.553
  783.3 8.6 %convolution_bitcast_fusion = f32[3,384,640]{1,2,0:T(8,128)S(1)} fusion(f32[3,512,640]{2,1,0:T(8,128)} %reshape.553, f32[256,384]{1,0:T(8,128)S(1)} %get-tuple-element.68, f32[256,384]{1,0:T(8,128)S(1)} %copy-done.6), kind=kOutput, calls=%fused_computation.2 | convolution fusion | flops 4530241536 | bytes 7667712 | tf_op jit(solution)/shard_map/tc,kcx->ktx/dot_general | solution.py:141
  793.5 2.5 convolution_bitcast_fusion.2
  797.0 44.3 %all_to_all.67 = f32[2,256,5,1,128]{4,0,3,2,1:T(2,128)S(1)} all-to-all(f32[2,256,5,1,128]{4,0,3,2,1:T(2,128)S(1)} %copy.123), channel_id=1, replica_groups=mesh['freq'=128,'plane'=2] {'freq'}, dimensions={1} | all-to-all | bytes 2621440 | tf_op jit(solution)/shard_map/all_to_all | solution.py:151
  841.3 1.2 copy.140
  (105 shorter events, 32.5 us)
Async XLA Ops:
  7.2 5.4 copy-start
  7.2 207.8 %all-gather.5.cloned.1.call-start = ((), (), s32[]{:S(2)}) async-start(), calls=%async_computation.5 | async-start | bytes 42270720 | tf_op jit(solution)/shard_map/all_gather | solution.py:19
  11.8 406.9 %all-gather.3.cloned.1.call-start = ((), (), s32[]{:S(2)}) async-start(), calls=%async_computation.4 | async-start | bytes 42270720 | tf_op jit(solution)/shard_map/all_gather | solution.py:19
  12.5 421.3 %collective-permute-start.1 = (f32[2,2,5,1,128]{4,3,2,1,0:T(1,128)S(1)}, f32[2,2,5,1,128]{4,3,2,1,0:T(1,128)S(1)}, u32[]{:S(2)}, u32[]{:S(2)}) collective-permute-start(f32[2,2,5,1,128]{4,3,2,1,0:T(1,128)S(1)} %get-tuple-element.55), channel_id=1, source_target_pairs={{0,1},{1,0},{2,3},{3,2},{4,5},{5,4},{6,7},{7,6},{8,9},{9,8},{10,11... | collective-permute-start | bytes 30728 | tf_op jit(solution)/shard_map/ppermute | solution.py:29
  14.5 419.4 %collective-permute-start = (f32[2,2,5,1,128]{4,3,2,1,0:T(1,128)S(1)}, f32[2,2,5,1,128]{4,3,2,1,0:T(1,128)S(1)}, u32[]{:S(2)}, u32[]{:S(2)}) collective-permute-start(f32[2,2,5,1,128]{4,3,2,1,0:T(1,128)S(1)} %get-tuple-element.54), channel_id=1, source_target_pairs={{1,0},{0,1},{3,2},{2,3},{5,4},{4,5},{7,6},{6,7},{9,8},{8,9},{11,10... | collective-permute-start | bytes 30728 | tf_op jit(solution)/shard_map/ppermute | solution.py:31
  433.5 1.3 copy-start.2
  436.6 3.9 collective-permute-start.3
  437.2 4.1 collective-permute-start.2
  443.2 3.8 collective-permute-start.5
  444.8 3.7 collective-permute-start.4
  450.3 3.8 collective-permute-start.7
  451.0 3.7 collective-permute-start.6
  456.4 3.8 collective-permute-start.8
  458.0 3.8 collective-permute-start.9
  467.4 85.7 %all-to-all-start = ((f32[3,2,2,5,128,128]{5,2,3,1,0,4:T(2,128)}), f32[3,2,2,5,128,128]{5,2,3,1,0,4:T(2,128)}, u32[]{:S(2)}, u32[]{:S(2)}) async-start(f32[3,2,2,5,128,128]{5,2,3,1,0,4:T(2,128)} %copy.114), calls=%async_computation | async-start | bytes 7864320 | tf_op jit(solution)/shard_map/all_to_all | solution.py:140
  480.7 84.8 %copy-start.5 = (f32[256,384]{1,0:T(8,128)}, f32[256,384]{1,0:T(8,128)S(1)}, u32[]{:S(2)}) copy-start(f32[256,384]{1,0:T(8,128)S(1)} %get-tuple-element.69) | copy-start | bytes 1179652
  480.8 93.9 %copy-start.3 = (f32[512,384]{1,0:T(8,128)}, f32[512,384]{1,0:T(8,128)S(1)}, u32[]{:S(2)}) copy-start(f32[512,384]{1,0:T(8,128)S(1)} %fusion.37) | copy-start | bytes 2359300
  579.3 56.7 %all-to-all-start.1 = ((f32[2,256,5,1,128]{4,0,3,2,1:T(2,128)}), f32[2,256,5,1,128]{4,0,3,2,1:T(2,128)S(1)}, u32[]{:S(2)}, u32[]{:S(2)}) async-start(f32[2,256,5,1,128]{4,0,3,2,1:T(2,128)} %copy.117), calls=%async_computation.1 | async-start | bytes 2621440 | tf_op jit(solution)/shard_map/all_to_all | solution.py:151
  639.0 9.0 %collective-permute-start.11 = (f32[2,2,5,1,128]{4,3,2,1,0:T(1,128)S(1)}, f32[2,2,5,1,128]{4,3,2,1,0:T(1,128)S(1)}, u32[]{:S(2)}, u32[]{:S(2)}) collective-permute-start(f32[2,2,5,1,128]{4,3,2,1,0:T(1,128)S(1)} %get-tuple-element.37), channel_id=1, source_target_pairs={{0,1},{1,0},{2,3},{3,2},{4,5},{5,4},{6,7},{7,6},{8,9},{9,8},{10,11... | collective-permute-start | bytes 30728 | tf_op jit(solution)/shard_map/ppermute | solution.py:29
  646.3 3.7 collective-permute-start.10
  651.8 3.8 collective-permute-start.13
  652.0 3.7 collective-permute-start.12
  657.5 3.8 collective-permute-start.15
  659.5 3.9 collective-permute-start.14
  665.1 4.2 copy-start.1
  665.1 3.8 collective-permute-start.17
  665.2 3.8 collective-permute-start.16
  776.4 6.9 copy-start.6
  792.3 1.1 copy-start.4
Sparse Core Ops, SparseCore 0:
  12.2 202.7 all-gather.4
  219.1 199.5 all-gather.2
